TPU v7x, 128 devices: a whole 4x4x4 slice. The times are simulated.
128 devices in a mesh: dp: 8 (over x, core), ctx: 4 (over y), tensor: 4 (over z).
Axes of the slice: x: 4, y: 4, z: 4, core: 2. Of those that a mesh axis runs over, the one named last changes fastest.
Arguments:
- hidden: bfloat16 [8, 16384, 2560], P('dp', 'ctx', 'tensor'), may hold values from -6 to 6
- depth: int32 [8, 16384], P('dp', 'ctx'), may hold values from 1 to 4, as said below
- qkv_weight: bfloat16 [2560, 3, 2560], P(None, None, 'tensor'), may hold values from -0.125 to 0.125
- out_weight: bfloat16 [2560, 2560], P('tensor'), may hold values from -0.125 to 0.125
Outputs:
- update: bfloat16 [8, 16384, 2560], P('dp', 'ctx', 'tensor')
Inputs may be any that keep to these rules, and one draw needn't show every extreme that they name: In every aligned block of 4096 positions of a document at most 1024 tokens have depth at least 3, and some block has exactly 1024; over all documents exactly 16384 tokens do.
All inputs are finite; a program needn't handle non-finite values.
Results may differ from a plain program's by a relative error of at most 0.012.
The roundings to bfloat16 on the way count: a program that leaves them out, or rounds other values in their place, can miss the bound.
Values may be sent and summed in bfloat16 or wider, within the bound.
No kernel may reach another device: no remote copies, remote signals or barrier semaphores. Data moves between devices by JAX's collectives and lax.ppermute only.
A program may use at most 256 MiB of HBM per device.

v0:
```python
import jax
import jax.numpy as jnp
from jax import lax
from jax.sharding import PartitionSpec as P

HD = 128
RECURSION = 3
ACT_DEV = 512
CAP = 1024
score_scale = 0.25
norm_epsilon = 1e-05
head_epsilon = 1e-06


def head_normed(values):
    row_count = values.shape[0]
    per_head = values.reshape(row_count, -1, HD)
    factor = lax.rsqrt(jnp.mean(per_head * per_head, axis=2, keepdims=True) + head_epsilon)
    return (per_head * factor).reshape(row_count, -1).astype(jnp.bfloat16)


def project_rows(token_rows, qkv_weight):
    full_rows = lax.all_gather(token_rows, "tensor", axis=1, tiled=True)
    widened = full_rows.astype(jnp.float32)
    factor = lax.rsqrt(jnp.mean(widened * widened, axis=1, keepdims=True) + norm_epsilon)
    normed = (widened * factor).astype(jnp.bfloat16)
    head_width = qkv_weight.shape[2]
    projection = jnp.dot(
        normed,
        qkv_weight.reshape(qkv_weight.shape[0], 3 * head_width),
        preferred_element_type=jnp.float32,
    )
    queries = head_normed(projection[:, :head_width])
    keys_normed = head_normed(projection[:, head_width : 2 * head_width])
    values_out = projection[:, 2 * head_width :].astype(jnp.bfloat16)
    return jnp.concatenate([queries, keys_normed, values_out], axis=1)


def output_rows(context, out_weight):
    partial_value = jnp.dot(context, out_weight, preferred_element_type=jnp.float32)
    return lax.psum_scatter(
        partial_value.astype(jnp.bfloat16), "tensor", scatter_dimension=1, tiled=True
    )


def move_tiles(payload):
    return lax.all_to_all(payload, ("dp", "ctx"), split_axis=0, concat_axis=0, tiled=True)


def per_device(hidden, depth, qkv_weight, out_weight):
    tokens = hidden[0]
    local_len = tokens.shape[0]
    feature_width = tokens.shape[1]
    capacity = CAP
    head_width = out_weight.shape[0]
    heads_here = head_width // HD
    ctx_count = lax.axis_size("ctx")
    spread_size = lax.axis_size("dp") * ctx_count
    ctx_rank = lax.axis_index("ctx")
    my_index = lax.axis_index("dp") * ctx_count + ctx_rank
    active = (depth[0] >= RECURSION).astype(jnp.int32)
    active_count = jnp.sum(active)
    active_rank = jnp.cumsum(active) - 1
    slot_token = (
        jnp.zeros((capacity,), jnp.int32)
        .at[jnp.where(active > 0, active_rank, capacity)]
        .set(jnp.arange(local_len, dtype=jnp.int32), mode="drop")
    )
    filled = jnp.arange(capacity, dtype=jnp.int32) < active_count
    token_rows = jnp.where(filled[:, None], tokens[slot_token], jnp.zeros((), tokens.dtype))
    counts = lax.all_gather(active_count[None], ("dp", "ctx"), axis=0, tiled=True)
    doc_counts = lax.dynamic_slice_in_dim(counts, lax.axis_index("dp") * ctx_count, ctx_count)
    slot_size = capacity // spread_size
    offsets = jnp.cumsum(counts) - counts
    first_rank = offsets[my_index]
    global_rank = first_rank + jnp.arange(capacity, dtype=jnp.int32)
    target = global_rank % spread_size
    position = (
        global_rank // spread_size
        - first_rank // spread_size
        - (target < first_rank % spread_size).astype(jnp.int32)
    )
    send_at = jnp.where(filled, target * slot_size + position, capacity)
    fetch_at = jnp.minimum(send_at, capacity - 1)
    lower_bound = (offsets - my_index + spread_size - 1) // spread_size
    upper_bound = (offsets + counts - my_index + spread_size - 1) // spread_size
    arrived = (
        jnp.arange(slot_size, dtype=jnp.int32)[None, :] < (upper_bound - lower_bound)[:, None]
    ).reshape(-1)
    arrived_rank = jnp.cumsum(arrived.astype(jnp.int32)) - 1
    chosen = (
        jnp.zeros((ACT_DEV,), jnp.int32)
        .at[jnp.where(arrived, arrived_rank, ACT_DEV)]
        .set(jnp.arange(capacity, dtype=jnp.int32), mode="drop")
    )
    packed = (
        jnp.zeros((capacity,) + token_rows.shape[1:], token_rows.dtype)
        .at[send_at]
        .set(token_rows, mode="drop")
    )
    values = project_rows(move_tiles(packed)[chosen], qkv_weight)
    bring_packed = jnp.zeros((capacity,) + values.shape[1:], values.dtype).at[chosen].set(values)
    projected = move_tiles(bring_packed)[fetch_at]
    queries = projected[:, :head_width]
    key_values = projected[:, head_width:]
    query_heads = queries.reshape(capacity, heads_here, HD)
    key_piece = lax.all_gather(key_values, "ctx", axis=0, tiled=True)
    piece_rows = key_piece.shape[0]
    row_index = jnp.arange(piece_rows, dtype=jnp.int32)
    source_shard = row_index // capacity
    source_slot = row_index - source_shard * capacity
    clipped = jnp.clip(source_shard, 0, ctx_count - 1)
    key_filled = (source_shard >= 0) & (source_slot < doc_counts[clipped])
    same_block = (source_shard == ctx_rank)[None, :] & (
        slot_token[source_slot][None, :] <= slot_token[:, None]
    )
    earlier = (source_shard < ctx_rank)[None, :] | same_block
    allowed = earlier & key_filled[None, :] & filled[:, None]
    key_heads = key_piece[:, :head_width].reshape(piece_rows, heads_here, HD)
    value_heads = key_piece[:, head_width:].reshape(piece_rows, heads_here, HD)
    scores = (
        jnp.einsum("qhd,khd->hqk", query_heads, key_heads, preferred_element_type=jnp.float32)
        * score_scale
    )
    weights = jnp.where(allowed[None], jnp.exp(scores), 0.0)
    numerator = jnp.einsum(
        "hqk,khd->qhd",
        weights.astype(jnp.bfloat16),
        value_heads,
        preferred_element_type=jnp.float32,
    )
    denominator = jnp.sum(weights, axis=2)
    numerator, denominator = (numerator, denominator)
    guarded = denominator + (1.0 - filled.astype(jnp.float32))[None, :]
    context = (
        (numerator / jnp.transpose(guarded)[:, :, None])
        .reshape(capacity, head_width)
        .astype(jnp.bfloat16)
    )
    result_rows = output_rows(context, out_weight)
    update = (
        jnp.zeros((local_len, feature_width), jnp.bfloat16)
        .at[jnp.where(filled, slot_token, local_len)]
        .set(result_rows, mode="drop")
    )
    return update[None]


def solution(mesh):
    placed = (P("dp", "ctx", "tensor"), P("dp", "ctx"), P(None, None, "tensor"), P("tensor", None))
    return jax.shard_map(
        per_device, mesh=mesh, in_specs=placed, out_specs=P("dp", "ctx", "tensor"), check_vma=False
    )
```

profile of v0, /device:TPU:1, one launch (start us, length us, event | category | flops | bytes accessed | tf_op | source)
XLA Modules:
  0.0 554.3 jit_solution(16296913542401398679)
XLA Ops:
  6.5 0.9 compare_convert_fusion
  7.4 1.5 fusion.45
  9.0 1.2 dynamic-slice
  10.2 1.4 dynamic-update-slice
  11.6 16.9 %all-reduce = s32[32]{0:T(128)S(1)} all-reduce(s32[32]{0:T(128)S(1)} %dynamic-update-slice), channel_id=1, replica_groups=mesh['dp'=8,'ctx'=4,'tensor'=4] {'dp','ctx'}, use_global_device_ids=true, to_apply=%add | all-reduce | flops 32 | bytes 256
  28.5 0.1 copy.18
  28.6 0.1 reduce.2
  28.8 0.6 dynamic_slice.6
  31.9 0.6 iota_compare_fusion.1
  32.6 0.3 reduce-window.31
  33.0 0.1 slice_reduce_fusion
  33.2 0.8 compare_select_fusion.2
  33.9 15.5 %scatter_custom_fusion = s32[1024]{0:T(1024)S(1)} fusion(s32[4096]{0:T(1024)S(1)} %bitcast.67, s32[4096]{0:T(1024)S(1)} %iota.52, s32[]{:T(128)} %constant.133.clone.1), kind=kCustom, calls=%fused_computation.99 | custom fusion | bytes 4100 | tf_op jit(solution)/shard_map/scatter | solution.py:67
  49.5 1.2 fusion.34
  50.7 1.3 compare_select_fusion.6
  52.0 37.8 %scatter_custom_fusion.2 = bf16[1024,640]{1,0:T(8,128)(2,1)} fusion(s32[1024]{0:T(1024)S(1)} %bitcast.71, pred[1024]{0:T(1024)(128)(4,1)S(1)} %iota_compare_fusion.1, bf16[]{:T(256)} %constant.131.clone.1, bf16[4096,640]{1,0:T(8,128)(2,1)} %bitcast.59, s32[1024]{0:T(1024)S(1)} %get-tuple-element.13), kind=kCustom, calls=%fused_computation.37 | custom fusion | flops 655360 | bytes 6559744 | tf_op jit(solution)/shard_map/scatter | solution.py:99
  89.8 12.2 %all-to-all-start = ((bf16[32,32,640]{2,1,0:T(8,128)(2,1)}), bf16[32,32,640]{2,1,0:T(8,128)(2,1)}, u32[]{:S(2)}, u32[]{:S(2)}) async-start(bf16[32,32,640]{2,1,0:T(8,128)(2,1)} %bitcast.60), calls=%async_computation | async-start | bytes 2621440 | tf_op jit(solution)/shard_map/all_to_all | solution.py:47
  102.2 0.1 lt.196
  102.3 0.1 lt.202
  102.4 0.1 lt.198
  102.5 0.3 reduce-window.34
  102.9 0.1 slice_reduce_fusion.1
  103.1 4.8 scatter_custom_fusion.1
  107.9 13.0 %all-to-all-done = bf16[32,32,640]{2,1,0:T(8,128)(2,1)} async-done(((bf16[32,32,640]{2,1,0:T(8,128)(2,1)}), bf16[32,32,640]{2,1,0:T(8,128)(2,1)}, u32[]{:S(2)}, u32[]{:S(2)}) %all-to-all-start) | async-done | bytes 1310752 | tf_op jit(solution)/shard_map/all_to_all | solution.py:47
  120.9 4.3 gather_fusion
  125.2 13.9 %copy.19 = bf16[2560,3,640]{0,2,1:T(8,128)(2,1)} copy(bf16[2560,3,640]{2,0,1:T(8,128)(2,1)} %param.6) | data formatting | bytes 19660800 | tf_op args[2]
  139.1 21.1 %all-gather.6.cloned.1.call-done = bf16[512,2560]{1,0:T(8,128)(2,1)} async-done(((bf16[512,640]{1,0:T(8,128)(2,1)}), bf16[512,2560]{1,0:T(8,128)(2,1)}) %all-gather.6.cloned.1.call-update) | async-done | bytes 2621456 | tf_op jit(solution)/shard_map/all_gather | solution.py:23
  160.2 2.3 fusion.5
  162.5 9.3 %fusion.7 = f32[512,1920]{1,0:T(8,128)S(1)} fusion(bf16[2560,1920]{0,1:T(8,128)(2,1)} %bitcast.52, bf16[512,2560]{1,0:T(8,128)(2,1)} %all-gather.6.cloned.1.call-done, f32[512]{0:T(512)S(1)} %add_rsqrt_fusion.2), kind=kOutput, calls=%fused_computation.20 | convolution fusion | flops 5037096960 | bytes 16386048 | tf_op jit(solution)/shard_map/dot_general | solution.py:28
  171.8 1.0 slice.81
  172.8 1.2 copy-done.1
  174.0 1.7 slice_multiply_fusion.1
  175.7 2.8 copy.20
  178.5 1.4 reduce_sum.47
  179.9 1.2 mul.93
  181.2 2.8 copy.21
  183.9 2.8 copy.22
  186.8 1.4 reduce_sum.48
  188.2 1.2 mul.98
  189.5 2.8 copy.23
  192.3 3.8 multiply_convert_fusion.1
  196.1 7.0 %scatter_custom_fusion.3 = bf16[1024,1920]{1,0:T(8,128)(2,1)} fusion(s32[512]{0:T(512)S(1)} %compare_select_fusion.15, bf16[512,640]{1,0:T(8,128)(2,1)} %slice.81, bf16[]{:T(256)} %constant.171, bf16[512,640]{1,0:T(8,128)(2,1)} %get-tuple-element.10, bf16[512,640]{1,0:T(8,128)(2,1)} %get-tuple-element.9, bf16[]{:T(256)} %constant.131.clone.1), kind=kCustom, calls=%fused_computation.26 | custom fusion | flops 5898240 | bytes 5898244 | tf_op jit(solution)/shard_map/scatter | solution.py:102
  203.1 7.7 %all-to-all-start.1 = ((bf16[32,32,1920]{2,1,0:T(8,128)(2,1)}), bf16[32,32,1920]{2,1,0:T(8,128)(2,1)}, u32[]{:S(2)}, u32[]{:S(2)}) async-start(bf16[32,32,1920]{2,1,0:T(8,128)(2,1)} %bitcast.51), calls=%async_computation.1 | async-start | bytes 7864320 | tf_op jit(solution)/shard_map/all_to_all | solution.py:47
  210.9 47.3 %all-to-all-done.1 = bf16[32,32,1920]{2,1,0:T(8,128)(2,1)} async-done(((bf16[32,32,1920]{2,1,0:T(8,128)(2,1)}), bf16[32,32,1920]{2,1,0:T(8,128)(2,1)}, u32[]{:S(2)}, u32[]{:S(2)}) %all-to-all-start.1) | async-done | bytes 3932192 | tf_op jit(solution)/shard_map/all_to_all | solution.py:47
  258.2 11.1 %gather_fusion.1 = bf16[1024,1920]{1,0:T(8,128)(2,1)} fusion(bf16[1024,1920]{1,0:T(8,128)(2,1)} %bitcast.20, s32[1024]{0:T(1024)S(1)} %broadcast_clamp_fusion.1), kind=kCustom, calls=%fused_computation.2 | custom fusion | bytes 7868416 | tf_op jit(solution)/shard_map/gather | solution.py:103
  269.3 3.4 slice.66
  272.8 16.7 %gather_fusion.2 = s32[4096]{0:T(1024)S(1)} fusion(s32[1024]{0:T(1024)S(1)} %scatter_custom_fusion, s32[4096]{0:T(1024)S(1)} %broadcast_clamp_fusion), kind=kCustom, calls=%fused_computation.3 | custom fusion | bytes 49152 | tf_op jit(solution)/shard_map/gather | solution.py:115
  289.6 0.6 convert_subtract_fusion
  290.3 0.6 fusion.47
  290.9 2.4 compare_select_fusion.3
  293.3 6.2 %and_and_fusion = pred[1024,4096]{1,0:T(8,128)(4,1)} fusion(s32[4096]{0:T(1024)S(1)} %gather_fusion.2, s32[1024]{0:T(1024)S(1)} %scatter_custom_fusion, pred[1024]{0:T(1024)(128)(4,1)S(1)} %iota_compare_fusion.1, pred[4096]{0:T(1024)(128)(4,1)S(1)} %fusion.32, pred[4096]{0:T(1024)(128)(4,1)S(1)} %get-tuple-element.23, pred[4096]{0:T(1024)(128)(4,1)S(1)} %get-tuple-element.24), kind=kLoop, calls=%fused_computation.14 | loop fusion | flops 20971520 | bytes 4228096 | tf_op jit(solution)/shard_map/and | solution.py:118
  299.5 2.5 slice.68
  302.1 2.5 copy.25
  304.5 69.3 %all-gather.4.cloned.1.call-done = bf16[4096,1280]{1,0:T(8,128)(2,1)} async-done(((bf16[1024,1280]{1,0:T(8,128)(2,1)}), bf16[4096,1280]{1,0:T(8,128)(2,1)}) %all-gather.4.cloned.1.call-update) | async-done | bytes 10485776 | tf_op jit(solution)/shard_map/all_gather | solution.py:107
  373.8 9.0 %fusion.46 = (bf16[4096,640]{1,0:T(8,128)(2,1)}, bf16[4096,640]{1,0:T(8,128)(2,1)}) fusion(bf16[4096,1280]{1,0:T(8,128)(2,1)} %all-gather.4.cloned.1.call-done), kind=kLoop, calls=%fused_computation.116 | loop fusion | bytes 20971520 | tf_op jit(solution)/shard_map/slice | solution.py:119
  382.8 7.9 %copy.24 = bf16[4096,640]{0,1:T(8,128)(2,1)} copy(bf16[4096,640]{1,0:T(8,128)(2,1)} %get-tuple-element.8) | data formatting | bytes 10485760 | tf_op jit(solution)/shard_map/slice | solution.py:120
  390.8 8.0 %copy.26 = bf16[4096,640]{0,1:T(8,128)(2,1)} copy(bf16[4096,640]{1,0:T(8,128)(2,1)} %get-tuple-element.7) | data formatting | bytes 10485760 | tf_op jit(solution)/shard_map/slice | solution.py:119
  398.8 36.3 %fusion = (f32[5,1024]{1,0:T(8,128)S(1)}, f32[5,1024,4096]{2,1,0:T(8,128)}) fusion(pred[1024,4096]{1,0:T(8,128)(4,1)} %and_and_fusion, bf16[1024,5,128]{0,2,1:T(8,128)(2,1)} %bitcast.61, bf16[4096,5,128]{0,2,1:T(8,128)(2,1)} %bitcast.54), kind=kOutput, calls=%fused_computation.10 | convolution fusion | flops 5431618560 | bytes 94654464 | tf_op jit(solution)/shard_map/qhd,khd->hqk/dot_general | solution.py:122
  435.1 30.0 %fusion.9 = bf16[1024,5,128]{0,2,1:T(8,128)(2,1)S(1)} fusion(bf16[4096,5,128]{0,2,1:T(8,128)(2,1)} %bitcast.53, f32[5,1024,4096]{2,1,0:T(8,128)} %get-tuple-element.20, pred[1024,4096]{1,0:T(8,128)(4,1)} %and_and_fusion, f32[1024,5]{0,1:T(8,128)S(1)} %add_bitcast_fusion), kind=kOutput, calls=%fused_computation.22 | convolution fusion | flops 5432934400 | bytes 94654464 | tf_op jit(solution)/shard_map/hqk,khd->qhd/dot_general | solution.py:126
  465.1 6.3 %convolution_convert_fusion = bf16[1024,2560]{1,0:T(8,128)(2,1)} fusion(bf16[1024,640]{0,1:T(8,128)(2,1)S(1)} %bitcast.73, bf16[640,2560]{1,0:T(8,128)(2,1)S(1)} %copy-done), kind=kOutput, calls=%fused_computation.17 | convolution fusion | flops 3358064640 | bytes 9830400 | tf_op jit(solution)/shard_map/dot_general | solution.py:40
  471.4 8.0 %copy.31 = bf16[1024,2560]{0,1:T(8,128)(2,1)} copy(bf16[1024,2560]{1,0:T(8,128)(2,1)} %convolution_convert_fusion) | data formatting | bytes 10485760
  479.4 56.8 %reduce-scatter.4.cloned.1.call-done = bf16[640,1024]{1,0:T(8,128)(2,1)} async-done(((bf16[2560,1024]{1,0:T(8,128)(2,1)}), bf16[640,1024]{1,0:T(8,128)(2,1)}) %reduce-scatter.4.cloned.1.call-update) | async-done | bytes 1310736
  536.2 2.4 copy.32
  538.6 9.0 %scatter_custom_fusion.4 = bf16[4096,640]{1,0:T(8,128)(2,1)} fusion(s32[1024]{0:T(1024)} %get-tuple-element.14, bf16[1024,640]{1,0:T(8,128)(2,1)} %copy.32, bf16[]{:T(256)} %constant.131.clone.1), kind=kCustom, calls=%fused_computation.24 | custom fusion | bytes 5243392 | tf_op jit(solution)/shard_map/scatter | solution.py:144
  (38 shorter events, 1.1 us)
Async XLA Ops:
  6.5 458.6 %copy-start = (bf16[640,2560]{1,0:T(8,128)(2,1)S(1)}, bf16[640,2560]{1,0:T(8,128)(2,1)}, u32[]{:S(2)}) copy-start(bf16[640,2560]{1,0:T(8,128)(2,1)} %param.7) | copy-start | bytes 9830404
  89.8 31.1 %all-to-all-start = ((bf16[32,32,640]{2,1,0:T(8,128)(2,1)}), bf16[32,32,640]{2,1,0:T(8,128)(2,1)}, u32[]{:S(2)}, u32[]{:S(2)}) async-start(bf16[32,32,640]{2,1,0:T(8,128)(2,1)} %bitcast.60), calls=%async_computation | async-start | bytes 2621440 | tf_op jit(solution)/shard_map/all_to_all | solution.py:47
  102.0 58.2 %all-gather.6.cloned.1.call-start = ((), (), s32[]{:S(2)}) async-start(), calls=%async_computation.4 | async-start | bytes 3276800 | tf_op jit(solution)/shard_map/all_gather | solution.py:23
  171.8 2.1 copy-start.1
  203.1 55.1 %all-to-all-start.1 = ((bf16[32,32,1920]{2,1,0:T(8,128)(2,1)}), bf16[32,32,1920]{2,1,0:T(8,128)(2,1)}, u32[]{:S(2)}, u32[]{:S(2)}) async-start(bf16[32,32,1920]{2,1,0:T(8,128)(2,1)} %bitcast.51), calls=%async_computation.1 | async-start | bytes 7864320 | tf_op jit(solution)/shard_map/all_to_all | solution.py:47
  210.8 163.0 %all-gather.4.cloned.1.call-start = ((), (), s32[]{:S(2)}) async-start(), calls=%async_computation.3 | async-start | bytes 13107200 | tf_op jit(solution)/shard_map/all_gather | solution.py:107
  272.7 263.4 %reduce-scatter.4.cloned.1.call-start = ((), (), s32[]{:S(2)}) async-start(), calls=%async_computation.5 | async-start | bytes 6553600
Sparse Core Ops, SparseCore 0:
  125.4 34.7 all-gather.5
  272.9 100.8 all-gather.3
  479.5 56.6 reduce-scatter.3
where the time goes:
time: 563 us; the launch traced here: 554 us
  waiting for transfers between devices  208 us (37%)
  local copies, waits for them, and re-layouts  140 us (25%)
  matrix products  81.8 us (15%)
  other arithmetic  72.3 us (13%)
  starting transfers between devices  20 us (4%)
  blocking collectives  16.9 us (3%)
  between operations  16.2 us (3%)
    all_gather x1, waiting for transfers between devices, per_device(): key_piece = lax.all_gather(key_values, 'ctx', axis=0, tiled=True)  69.3 us
    all_to_all x2, waiting for transfers between devices, move_tiles(): lax.all_to_all(payload, ('dp', 'ctx'), split_axis=0, concat_axis=0, tiled...  60.3 us
    unnamed x4, waiting for transfers between devices  56.9 us
    scatter x1, other arithmetic, per_device(): packed = jnp.zeros((capacity,) + token_rows.shape[1:], token_rows.dtype)....  37.8 us
    dot_general x1, matrix products, per_device(): jnp.einsum('qhd,khd->hqk', query_heads, key_heads, preferred_element_type...  36.3 us
    dot_general x1, matrix products, per_device(): jnp.einsum('hqk,khd->qhd', weights.astype(jnp.bfloat16), value_heads, pre...  30 us
    unnamed x10, local copies, waits for them, and re-layouts  28 us
    all_gather x1, waiting for transfers between devices, project_rows(): full_rows = lax.all_gather(token_rows, 'tensor', axis=1, tiled=True)  21.1 us
  transfers between devices with their start and end apart: 5, of which 5 were waited for; matrix products, arithmetic and copies ran while one was open for 9% of the time, Pallas kernels for 0%

commit v1 on v0

--- a/solution.py
+++ b/solution.py
@@ -104,7 +104,9 @@
     queries = projected[:, :head_width]
     key_values = projected[:, head_width:]
     query_heads = queries.reshape(capacity, heads_here, HD)
-    key_piece = lax.all_gather(key_values, "ctx", axis=0, tiled=True)
+    key_piece = jnp.concatenate(
+        lax.all_to_all(jnp.stack([key_values] * lax.axis_size("ctx")), "ctx", 0, 0), axis=0
+    )
     piece_rows = key_piece.shape[0]
     row_index = jnp.arange(piece_rows, dtype=jnp.int32)
     source_shard = row_index // capacity

time: 563 us -> 588 us (1.044)
  waiting for transfers between devices: 208 us -> 220 us
  local copies, waits for them, and re-layouts: 140 us -> 146 us
  starting transfers between devices: 20 us -> 26 us
    all_to_all x0 -> x1, waiting for transfers between devices: none -> 83.1 us  [per_device(): lax.all_to_all(jnp.stack([key_values] * lax.axis_size('ctx')), 'ctx', 0, 0)]
    all_gather x1 -> x0, waiting for transfers between devices: 69.3 us -> none  [per_device(): key_piece = lax.all_gather(key_values, 'ctx', axis=0, tiled=True)]
    reshape x0 -> x1, local copies, waits for them, and re-layouts: none -> 9.67 us  [per_device(): jnp.concatenate(lax.all_to_all(jnp.stack([key_values] * lax.axis_size('ct...]
    slice x2 -> x1, local copies, waits for them, and re-layouts: 8.02 us -> 0.08 us  [the longest x1 7.94 us: per_device(): value_heads = key_piece[:, head_width:].reshape(piece_rows, heads_here, HD)]
    slice x2 -> x1, local copies, waits for them, and re-layouts: 17.1 us -> 9.78 us  [per_device(): key_heads = key_piece[:, :head_width].reshape(piece_rows, heads_here, HD)]
    another operation x4 -> x5, local copies, waits for them, and re-layouts: 0.39 us -> 7.5 us  [the longest x1 7.11 us: per_device(): jnp.stack([key_values] * lax.axis_size('ctx'))]
    all_to_all x0 -> x1, starting transfers between devices: none -> 5.99 us  [per_device(): lax.all_to_all(jnp.stack([key_values] * lax.axis_size('ctx')), 'ctx', 0, 0)]
    unnamed x4 -> x3, waiting for transfers between devices: 56.9 us -> 55.1 us
where the time goes in v1:
time: 588 us; the launch traced here: 579 us
  waiting for transfers between devices  220 us (37%)
  local copies, waits for them, and re-layouts  146 us (25%)
  matrix products  82.1 us (14%)
  other arithmetic  72.3 us (12%)
  starting transfers between devices  26 us (4%)
  blocking collectives  16.9 us (3%)
  between operations  16.5 us (3%)
    all_to_all x1, waiting for transfers between devices, per_device(): lax.all_to_all(jnp.stack([key_values] * lax.axis_size('ctx')), 'ctx', 0, 0)  83.1 us
    all_to_all x2, waiting for transfers between devices, move_tiles(): lax.all_to_all(payload, ('dp', 'ctx'), split_axis=0, concat_axis=0, tiled...  60.4 us
    unnamed x3, waiting for transfers between devices  55.1 us
    scatter x1, other arithmetic, per_device(): packed = jnp.zeros((capacity,) + token_rows.shape[1:], token_rows.dtype)....  37.8 us
    dot_general x1, matrix products, per_device(): jnp.einsum('qhd,khd->hqk', query_heads, key_heads, preferred_element_type...  36.3 us
    dot_general x1, matrix products, per_device(): jnp.einsum('hqk,khd->qhd', weights.astype(jnp.bfloat16), value_heads, pre...  30.4 us
    unnamed x10, local copies, waits for them, and re-layouts  28 us
    all_gather x1, waiting for transfers between devices, project_rows(): full_rows = lax.all_gather(token_rows, 'tensor', axis=1, tiled=True)  21.1 us
  transfers between devices with their start and end apart: 5, of which 5 were waited for; matrix products, arithmetic and copies ran while one was open for 9% of the time, Pallas kernels for 0%

profile of v1, /device:TPU:1, one launch (start us, length us, event | category | flops | bytes accessed | tf_op | source)
XLA Modules:
  0.0 579.2 jit_solution(11722300226851773190)
XLA Ops:
  6.5 0.9 compare_convert_fusion
  7.4 1.5 fusion.45
  9.0 1.2 dynamic-slice
  10.2 1.4 dynamic-update-slice
  11.6 16.9 %all-reduce = s32[32]{0:T(128)S(1)} all-reduce(s32[32]{0:T(128)S(1)} %dynamic-update-slice), channel_id=1, replica_groups=mesh['dp'=8,'ctx'=4,'tensor'=4] {'dp','ctx'}, use_global_device_ids=true, to_apply=%add | all-reduce | flops 32 | bytes 256
  28.5 0.1 copy.17
  28.6 0.1 reduce.2
  28.8 0.6 dynamic_slice.6
  31.9 0.6 iota_compare_fusion.1
  32.6 0.3 reduce-window.31
  33.0 0.1 slice_reduce_fusion
  33.2 0.8 compare_select_fusion.2
  33.9 15.5 %scatter_custom_fusion = s32[1024]{0:T(1024)S(1)} fusion(s32[4096]{0:T(1024)S(1)} %bitcast.70, s32[4096]{0:T(1024)S(1)} %iota.52, s32[]{:T(128)} %constant.133.clone.1), kind=kCustom, calls=%fused_computation.99 | custom fusion | bytes 4100 | tf_op jit(solution)/shard_map/scatter | solution.py:67
  49.5 1.2 fusion.34
  50.7 1.3 compare_select_fusion.6
  52.0 37.8 %scatter_custom_fusion.2 = bf16[1024,640]{1,0:T(8,128)(2,1)} fusion(s32[1024]{0:T(1024)S(1)} %bitcast.74, pred[1024]{0:T(1024)(128)(4,1)S(1)} %iota_compare_fusion.1, bf16[]{:T(256)} %constant.131.clone.1, bf16[4096,640]{1,0:T(8,128)(2,1)} %bitcast.62, s32[1024]{0:T(1024)S(1)} %get-tuple-element.13), kind=kCustom, calls=%fused_computation.37 | custom fusion | flops 655360 | bytes 6559744 | tf_op jit(solution)/shard_map/scatter | solution.py:99
  89.8 12.2 %all-to-all-start = ((bf16[32,32,640]{2,1,0:T(8,128)(2,1)}), bf16[32,32,640]{2,1,0:T(8,128)(2,1)}, u32[]{:S(2)}, u32[]{:S(2)}) async-start(bf16[32,32,640]{2,1,0:T(8,128)(2,1)} %bitcast.63), calls=%async_computation | async-start | bytes 2621440 | tf_op jit(solution)/shard_map/all_to_all | solution.py:47
  102.2 0.1 lt.196
  102.5 0.3 reduce-window.34
  102.9 0.1 slice_reduce_fusion.1
  103.1 4.8 scatter_custom_fusion.1
  107.9 13.0 %all-to-all-done = bf16[32,32,640]{2,1,0:T(8,128)(2,1)} async-done(((bf16[32,32,640]{2,1,0:T(8,128)(2,1)}), bf16[32,32,640]{2,1,0:T(8,128)(2,1)}, u32[]{:S(2)}, u32[]{:S(2)}) %all-to-all-start) | async-done | bytes 1310752 | tf_op jit(solution)/shard_map/all_to_all | solution.py:47
  120.9 4.3 gather_fusion
  125.3 13.9 %copy.18 = bf16[2560,3,640]{0,2,1:T(8,128)(2,1)} copy(bf16[2560,3,640]{2,0,1:T(8,128)(2,1)} %param.6) | data formatting | bytes 19660800 | tf_op args[2]
  139.1 21.1 %all-gather.3.cloned.1.call-done = bf16[512,2560]{1,0:T(8,128)(2,1)} async-done(((bf16[512,640]{1,0:T(8,128)(2,1)}), bf16[512,2560]{1,0:T(8,128)(2,1)}) %all-gather.3.cloned.1.call-update) | async-done | bytes 2621456 | tf_op jit(solution)/shard_map/all_gather | solution.py:23
  160.2 2.3 fusion.5
  162.6 9.2 %fusion.7 = f32[512,1920]{1,0:T(8,128)S(1)} fusion(bf16[2560,1920]{0,1:T(8,128)(2,1)} %bitcast.55, bf16[512,2560]{1,0:T(8,128)(2,1)} %all-gather.3.cloned.1.call-done, f32[512]{0:T(512)S(1)} %add_rsqrt_fusion.2), kind=kOutput, calls=%fused_computation.20 | convolution fusion | flops 5037096960 | bytes 16386048 | tf_op jit(solution)/shard_map/dot_general | solution.py:28
  171.8 1.0 slice.81
  172.8 1.1 copy-done.1
  173.9 1.7 slice_multiply_fusion.1
  175.6 2.8 copy.19
  178.4 1.4 reduce_sum.47
  179.9 1.2 mul.93
  181.1 2.8 copy.20
  183.9 2.8 copy.21
  186.7 1.4 reduce_sum.48
  188.2 1.2 mul.98
  189.4 2.8 copy.22
  192.2 3.8 multiply_convert_fusion.1
  196.0 7.0 %scatter_custom_fusion.3 = bf16[1024,1920]{1,0:T(8,128)(2,1)} fusion(s32[512]{0:T(512)S(1)} %compare_select_fusion.15, bf16[512,640]{1,0:T(8,128)(2,1)} %slice.81, bf16[]{:T(256)} %constant.171, bf16[512,640]{1,0:T(8,128)(2,1)} %get-tuple-element.10, bf16[512,640]{1,0:T(8,128)(2,1)} %get-tuple-element.9, bf16[]{:T(256)} %constant.131.clone.1), kind=kCustom, calls=%fused_computation.26 | custom fusion | flops 5898240 | bytes 5898244 | tf_op jit(solution)/shard_map/scatter | solution.py:102
  203.0 7.7 %all-to-all-start.1 = ((bf16[32,32,1920]{2,1,0:T(8,128)(2,1)}), bf16[32,32,1920]{2,1,0:T(8,128)(2,1)}, u32[]{:S(2)}, u32[]{:S(2)}) async-start(bf16[32,32,1920]{2,1,0:T(8,128)(2,1)} %bitcast.54), calls=%async_computation.1 | async-start | bytes 7864320 | tf_op jit(solution)/shard_map/all_to_all | solution.py:47
  210.8 47.4 %all-to-all-done.1 = bf16[32,32,1920]{2,1,0:T(8,128)(2,1)} async-done(((bf16[32,32,1920]{2,1,0:T(8,128)(2,1)}), bf16[32,32,1920]{2,1,0:T(8,128)(2,1)}, u32[]{:S(2)}, u32[]{:S(2)}) %all-to-all-start.1) | async-done | bytes 3932192 | tf_op jit(solution)/shard_map/all_to_all | solution.py:47
  258.2 11.1 %gather_fusion.1 = bf16[1024,1920]{1,0:T(8,128)(2,1)} fusion(bf16[1024,1920]{1,0:T(8,128)(2,1)} %bitcast.20, s32[1024]{0:T(1024)S(1)} %broadcast_clamp_fusion.1), kind=kCustom, calls=%fused_computation.2 | custom fusion | bytes 7868416 | tf_op jit(solution)/shard_map/gather | solution.py:103
  269.2 3.4 slice.66
  272.7 4.5 copy.23
  277.2 7.1 %stack.2 = bf16[4,1024,1280]{1,2,0:T(8,128)(2,1)} broadcast(bf16[1024,1280]{0,1:T(8,128)(2,1)} %copy.23), dimensions={1,2} | broadcast | bytes 13107200 | tf_op jit(solution)/shard_map/stack | solution.py:108
  284.3 6.0 %all-to-all-start.2 = ((bf16[4,1024,1280]{1,2,0:T(8,128)(2,1)}), bf16[4,1024,1280]{1,2,0:T(8,128)(2,1)}, u32[]{:S(2)}, u32[]{:S(2)}) async-start(bf16[4,1024,1280]{1,2,0:T(8,128)(2,1)} %stack.2), calls=%async_computation.2 | async-start | bytes 20971520 | tf_op jit(solution)/shard_map/all_to_all | solution.py:108
  290.4 16.7 %gather_fusion.2 = s32[4096]{0:T(1024)S(1)} fusion(s32[1024]{0:T(1024)S(1)} %scatter_custom_fusion, s32[4096]{0:T(1024)S(1)} %broadcast_clamp_fusion), kind=kCustom, calls=%fused_computation.3 | custom fusion | bytes 49152 | tf_op jit(solution)/shard_map/gather | solution.py:117
  307.2 0.6 convert_subtract_fusion
  307.8 0.7 fusion.47
  308.5 2.5 compare_select_fusion.3
  311.0 6.3 %and_and_fusion = pred[1024,4096]{1,0:T(8,128)(4,1)} fusion(s32[4096]{0:T(1024)S(1)} %gather_fusion.2, s32[1024]{0:T(1024)S(1)} %scatter_custom_fusion, pred[1024]{0:T(1024)(128)(4,1)S(1)} %iota_compare_fusion.1, pred[4096]{0:T(1024)(128)(4,1)S(1)} %fusion.32, pred[4096]{0:T(1024)(128)(4,1)S(1)} %get-tuple-element.23, pred[4096]{0:T(1024)(128)(4,1)S(1)} %get-tuple-element.24), kind=kLoop, calls=%fused_computation.14 | loop fusion | flops 20971520 | bytes 4228096 | tf_op jit(solution)/shard_map/and | solution.py:120
  317.3 2.5 slice.68
  319.8 2.5 copy.25
  322.3 83.1 %all-to-all-done.2 = bf16[4,1024,1280]{1,2,0:T(8,128)(2,1)} async-done(((bf16[4,1024,1280]{1,2,0:T(8,128)(2,1)}), bf16[4,1024,1280]{1,2,0:T(8,128)(2,1)}, u32[]{:S(2)}, u32[]{:S(2)}) %all-to-all-start.2) | async-done | bytes 10485792 | tf_op jit(solution)/shard_map/all_to_all | solution.py:108
  405.3 9.7 %copy.32 = bf16[4,160,8,1024]{3,2,0,1:T(8,128)(2,1)} copy(bf16[4,160,8,1024]{3,2,1,0:T(8,128)(2,1)} %bitcast.37) | data formatting | bytes 20971520 | tf_op jit(solution)/shard_map/reshape | solution.py:107
  415.0 9.8 %fusion.46 = (bf16[4096,640]{0,1:T(8,128)(2,1)}, bf16[4096,640]{0,1:T(8,128)(2,1)}) fusion(bf16[4096,1280]{0,1:T(8,128)(2,1)} %bitcast.52), kind=kLoop, calls=%fused_computation.116 | loop fusion | bytes 20971520 | tf_op jit(solution)/shard_map/slice | solution.py:121
  424.8 36.3 %fusion = (f32[5,1024]{1,0:T(8,128)S(1)}, f32[5,1024,4096]{2,1,0:T(8,128)}) fusion(pred[1024,4096]{1,0:T(8,128)(4,1)} %and_and_fusion, bf16[1024,5,128]{0,2,1:T(8,128)(2,1)} %bitcast.64, bf16[4096,5,128]{0,2,1:T(8,128)(2,1)} %bitcast.57), kind=kOutput, calls=%fused_computation.10 | convolution fusion | flops 5431618560 | bytes 94654464 | tf_op jit(solution)/shard_map/qhd,khd->hqk/dot_general | solution.py:124
  461.1 30.4 %fusion.9 = bf16[1024,5,128]{0,2,1:T(8,128)(2,1)S(1)} fusion(bf16[4096,5,128]{0,2,1:T(8,128)(2,1)} %bitcast.56, f32[5,1024,4096]{2,1,0:T(8,128)} %get-tuple-element.20, pred[1024,4096]{1,0:T(8,128)(4,1)} %and_and_fusion, f32[1024,5]{0,1:T(8,128)S(1)} %add_bitcast_fusion), kind=kOutput, calls=%fused_computation.22 | convolution fusion | flops 5432934400 | bytes 94654464 | tf_op jit(solution)/shard_map/hqk,khd->qhd/dot_general | solution.py:128
  491.5 6.1 %convolution_convert_fusion = bf16[1024,2560]{1,0:T(8,128)(2,1)} fusion(bf16[1024,640]{0,1:T(8,128)(2,1)S(1)} %bitcast.76, bf16[640,2560]{1,0:T(8,128)(2,1)S(1)} %copy-done), kind=kOutput, calls=%fused_computation.17 | convolution fusion | flops 3358064640 | bytes 9830400 | tf_op jit(solution)/shard_map/dot_general | solution.py:40
  497.6 8.0 %copy.30 = bf16[1024,2560]{0,1:T(8,128)(2,1)} copy(bf16[1024,2560]{1,0:T(8,128)(2,1)} %convolution_convert_fusion) | data formatting | bytes 10485760
  505.6 55.1 %reduce-scatter.4.cloned.1.call-done = bf16[640,1024]{1,0:T(8,128)(2,1)} async-done(((bf16[2560,1024]{1,0:T(8,128)(2,1)}), bf16[640,1024]{1,0:T(8,128)(2,1)}) %reduce-scatter.4.cloned.1.call-update) | async-done | bytes 1310736
  560.7 2.4 copy.31
  563.2 9.0 %scatter_custom_fusion.4 = bf16[4096,640]{1,0:T(8,128)(2,1)} fusion(s32[1024]{0:T(1024)} %get-tuple-element.14, bf16[1024,640]{1,0:T(8,128)(2,1)} %copy.31, bf16[]{:T(256)} %constant.131.clone.1), kind=kCustom, calls=%fused_computation.24 | custom fusion | bytes 5243392 | tf_op jit(solution)/shard_map/scatter | solution.py:146
  (38 shorter events, 1.2 us)
Async XLA Ops:
  6.5 485.0 %copy-start = (bf16[640,2560]{1,0:T(8,128)(2,1)S(1)}, bf16[640,2560]{1,0:T(8,128)(2,1)}, u32[]{:S(2)}) copy-start(bf16[640,2560]{1,0:T(8,128)(2,1)} %param.7) | copy-start | bytes 9830404
  89.8 31.1 %all-to-all-start = ((bf16[32,32,640]{2,1,0:T(8,128)(2,1)}), bf16[32,32,640]{2,1,0:T(8,128)(2,1)}, u32[]{:S(2)}, u32[]{:S(2)}) async-start(bf16[32,32,640]{2,1,0:T(8,128)(2,1)} %bitcast.63), calls=%async_computation | async-start | bytes 2621440 | tf_op jit(solution)/shard_map/all_to_all | solution.py:47
  102.0 58.2 %all-gather.3.cloned.1.call-start = ((), (), s32[]{:S(2)}) async-start(), calls=%async_computation.4 | async-start | bytes 3276800 | tf_op jit(solution)/shard_map/all_gather | solution.py:23
  171.8 2.1 copy-start.1
  203.0 55.1 %all-to-all-start.1 = ((bf16[32,32,1920]{2,1,0:T(8,128)(2,1)}), bf16[32,32,1920]{2,1,0:T(8,128)(2,1)}, u32[]{:S(2)}, u32[]{:S(2)}) async-start(bf16[32,32,1920]{2,1,0:T(8,128)(2,1)} %bitcast.54), calls=%async_computation.1 | async-start | bytes 7864320 | tf_op jit(solution)/shard_map/all_to_all | solution.py:47
  284.3 121.0 %all-to-all-start.2 = ((bf16[4,1024,1280]{1,2,0:T(8,128)(2,1)}), bf16[4,1024,1280]{1,2,0:T(8,128)(2,1)}, u32[]{:S(2)}, u32[]{:S(2)}) async-start(bf16[4,1024,1280]{1,2,0:T(8,128)(2,1)} %stack.2), calls=%async_computation.2 | async-start | bytes 20971520 | tf_op jit(solution)/shard_map/all_to_all | solution.py:108
  290.3 270.4 %reduce-scatter.4.cloned.1.call-start = ((), (), s32[]{:S(2)}) async-start(), calls=%async_computation.5 | async-start | bytes 6553600
Sparse Core Ops, SparseCore 0:
  125.4 34.7 all-gather.2
  505.7 54.9 reduce-scatter.3
